TPU v7x, 256 devices: a whole 4x4x8 slice. The times are simulated.
256 devices in a mesh: expert: 32 (over z, y), dp: 8 (over x, core).
Axes of the slice: x: 4, y: 4, z: 8, core: 2. Of those that a mesh axis runs over, the one named last changes fastest.
Arguments:
- tokens: bfloat16 [8192, 4096], P(('expert', 'dp')), may hold values from -6 to 6
- out_grad: bfloat16 [8192, 4096], P(('expert', 'dp')), may hold values from -6 to 6
- gate_probs: bfloat16 [8192, 8], P(('expert', 'dp')), may hold values from 0.049804688 to 0.5
- route_ids: int32 [8192, 8], P(('expert', 'dp')), may hold values from 0 to 127, all different within a row; in each aligned block of 32 rows (0 to 31, 32 to 63, ...) at most 4 rows name the same one
- w_gate: bfloat16 [32, 1536, 4096], P('expert', 'dp'), may hold values from -0.09375 to 0.09375
- w_up: bfloat16 [32, 1536, 4096], P('expert', 'dp'), may hold values from -0.09375 to 0.09375
- w_down: bfloat16 [32, 1536, 4096], P('expert', 'dp'), may hold values from -0.15625 to 0.15625
Outputs:
- token_grad: bfloat16 [8192, 4096], P(('expert', 'dp'))
- gate_grad: float32 [8192, 8], P(('expert', 'dp'))
- grad_gate: bfloat16 [32, 1536, 4096], P('expert', 'dp')
- grad_up: bfloat16 [32, 1536, 4096], P('expert', 'dp')
- grad_down: bfloat16 [32, 1536, 4096], P('expert', 'dp')
Inputs may be any that keep to these rules, and one draw needn't show every extreme that they name: `route_ids`: the 8 ids of a token differ. In each aligned block of 32 rows (the tokens of one device) no id is named by more than 4 rows, a bound that some block reaches.
All inputs are finite; a program needn't handle non-finite values.
Results may differ from a plain program's by a relative error of at most 0.014.
Values may be sent and summed in bfloat16 or wider, within the bound.
A program may use at most 128 MiB of HBM per device.

v0:
```python
import jax
import jax.numpy as jnp
from jax import lax
from jax.sharding import PartitionSpec as P

EXPERTS = 128
CAP = 4


CONTRACT_LAST = (((1,), (1,)), ((), ()))
CONTRACT_FIRST = (((0,), (0,)), ((), ()))


def route_table(route_ids, n_targets):
    per_device = EXPERTS // n_targets
    flat_ids = route_ids.reshape(-1)
    active = flat_ids % per_device == 0
    target = flat_ids // per_device
    onehot = jnp.logical_and(
        target[:, None] == jnp.arange(n_targets, dtype=jnp.int32)[None, :], active[:, None]
    ).astype(jnp.int32)
    slot_rank = jnp.sum((jnp.cumsum(onehot, axis=0) - onehot) * onehot, axis=1)
    slot_index = target * CAP + slot_rank
    placed = jnp.logical_and(
        slot_index[:, None] == jnp.arange(n_targets * CAP, dtype=jnp.int32)[None, :],
        active[:, None],
    )
    return placed.astype(jnp.float32).reshape(
        route_ids.shape[0], route_ids.shape[1], n_targets * CAP
    )


def dispatch_rows(routing, tokens, out_grad, gate_probs):
    picked = jnp.sum(routing, axis=1).astype(jnp.bfloat16)
    rows_token = lax.dot_general(
        picked, tokens, CONTRACT_FIRST, preferred_element_type=jnp.float32
    ).astype(jnp.bfloat16)
    rows_grad = lax.dot_general(
        picked, out_grad, CONTRACT_FIRST, preferred_element_type=jnp.float32
    ).astype(jnp.bfloat16)
    rows_gate = jnp.einsum(
        "tks,tk->s", routing, gate_probs.astype(jnp.float32), precision=lax.Precision.HIGHEST
    ).astype(jnp.bfloat16)
    return (rows_token, rows_grad, rows_gate)


def backward_rows(weights, portion):
    gate_weight, up_weight, down_weight = weights
    row_tokens, row_grads, row_gates = portion
    pre_gate = lax.dot_general(
        gate_weight, row_tokens, CONTRACT_LAST, preferred_element_type=jnp.float32
    )
    pre_up = lax.dot_general(
        up_weight, row_tokens, CONTRACT_LAST, preferred_element_type=jnp.float32
    )
    back_proj = lax.dot_general(
        down_weight, row_grads, CONTRACT_LAST, preferred_element_type=jnp.float32
    )
    squash = jax.nn.sigmoid(pre_gate)
    activated = pre_gate * squash
    hidden = (activated * pre_up).astype(jnp.bfloat16)
    gate_terms = jnp.sum(hidden.astype(jnp.float32) * back_proj, axis=0)
    gate_row = row_gates.astype(jnp.float32)
    out_scaled = (gate_row[:, None] * row_grads.astype(jnp.float32)).astype(jnp.bfloat16)
    hidden_grad = gate_row[None, :] * back_proj
    up_pre_grad = (hidden_grad * activated).astype(jnp.bfloat16)
    gate_pre_grad = (hidden_grad * pre_up * squash * (1.0 + pre_gate * (1.0 - squash))).astype(
        jnp.bfloat16
    )
    grad_down = jnp.dot(hidden, out_scaled, preferred_element_type=jnp.float32)
    grad_gate = jnp.dot(gate_pre_grad, row_tokens, preferred_element_type=jnp.float32)
    grad_up = jnp.dot(up_pre_grad, row_tokens, preferred_element_type=jnp.float32)
    return (grad_gate, grad_up, grad_down, gate_pre_grad, up_pre_grad, gate_terms)


def body(tokens, out_grad, gate_probs, route_ids, w_gate, w_up, w_down):
    n_targets = lax.axis_size("expert")
    n_members = lax.axis_size("dp")
    token_rows, model_width = tokens.shape
    top_count = route_ids.shape[1]
    slot_count = n_targets * CAP
    rows_total = n_members * slot_count
    weights = (w_gate[0], w_up[0], w_down[0])
    routing = route_table(route_ids, n_targets)
    group_rows = (
        lax.all_gather(tokens, "dp", axis=0, tiled=True),
        lax.all_gather(out_grad, "dp", axis=0, tiled=True),
        lax.all_gather(gate_probs, "dp", axis=0, tiled=True),
    )
    group_ids = lax.all_gather(route_ids, "dp", axis=0, tiled=True)

    def member_table(member_ids):
        return route_table(member_ids, n_targets)

    group_tables = jax.vmap(member_table)(group_ids.reshape(n_members, token_rows, top_count))
    outgoing = jax.vmap(dispatch_rows)(
        group_tables,
        group_rows[0].reshape(n_members, token_rows, model_width),
        group_rows[1].reshape(n_members, token_rows, model_width),
        group_rows[2].reshape(n_members, token_rows, top_count),
    )
    arrived = (
        lax.all_to_all(
            outgoing[0].reshape(n_members, n_targets, CAP, model_width),
            "expert",
            split_axis=1,
            concat_axis=1,
            tiled=True,
        ),
        lax.all_to_all(
            outgoing[1].reshape(n_members, n_targets, CAP, model_width),
            "expert",
            split_axis=1,
            concat_axis=1,
            tiled=True,
        ),
        lax.all_to_all(
            outgoing[2].reshape(n_members, n_targets, CAP),
            "expert",
            split_axis=1,
            concat_axis=1,
            tiled=True,
        ),
    )
    all_rows = (
        arrived[0].reshape(rows_total, model_width),
        arrived[1].reshape(rows_total, model_width),
        arrived[2].reshape(rows_total),
    )
    totals = backward_rows(weights, all_rows)
    grad_gate, grad_up, grad_down, gate_pre_all, up_pre_all, gate_terms_all = totals
    term = lax.dot_general(
        gate_pre_all, weights[0], CONTRACT_FIRST, preferred_element_type=jnp.float32
    )
    slot_grads = lax.psum_scatter(
        (
            term
            + lax.dot_general(
                up_pre_all, weights[1], CONTRACT_FIRST, preferred_element_type=jnp.float32
            )
        ).astype(jnp.bfloat16),
        "dp",
        scatter_dimension=0,
        tiled=True,
    ).astype(jnp.float32)
    slot_gates = lax.psum_scatter(gate_terms_all, "dp", scatter_dimension=0, tiled=True)
    returned = (
        lax.all_to_all(
            slot_grads.reshape(n_targets, CAP, model_width).astype(jnp.bfloat16),
            "expert",
            split_axis=0,
            concat_axis=0,
            tiled=True,
        ).astype(jnp.float32),
        lax.all_to_all(
            slot_gates.reshape(n_targets, CAP).astype(jnp.bfloat16),
            "expert",
            split_axis=0,
            concat_axis=0,
            tiled=True,
        ).astype(jnp.float32),
    )
    returned_rows = returned[0].reshape(slot_count, model_width)
    returned_gates = returned[1].reshape(slot_count)
    token_grad = jnp.dot(
        jnp.sum(routing, axis=1),
        returned_rows,
        precision=lax.Precision.HIGHEST,
        preferred_element_type=jnp.float32,
    )
    gate_grad = jnp.einsum("tks,s->tk", routing, returned_gates, precision=lax.Precision.HIGHEST)
    return (
        token_grad.astype(jnp.bfloat16),
        gate_grad,
        grad_gate.astype(jnp.bfloat16)[None],
        grad_up.astype(jnp.bfloat16)[None],
        grad_down.astype(jnp.bfloat16)[None],
    )


def solution(mesh):
    in_specs = (
        P(("expert", "dp"), None),
        P(("expert", "dp"), None),
        P(("expert", "dp"), None),
        P(("expert", "dp"), None),
        P("expert", "dp", None),
        P("expert", "dp", None),
        P("expert", "dp", None),
    )
    out_specs = (
        P(("expert", "dp"), None),
        P(("expert", "dp"), None),
        P("expert", "dp", None),
        P("expert", "dp", None),
        P("expert", "dp", None),
    )
    return jax.shard_map(body, mesh=mesh, in_specs=in_specs, out_specs=out_specs, check_vma=False)
```

profile of v0, /device:TPU:16, one launch (start us, length us, event | category | flops | bytes accessed | tf_op | source)
XLA Modules:
  0.0 642.4 jit_solution(15827697453292318851)
XLA Ops:
  7.2 0.7 all-gather.7.cloned.1.call-update
  7.9 13.4 %all-gather = s32[8,32,8]{1,2,0:T(8,128)S(1)} all-gather(s32[1,32,8]{1,2,0:T(8,128)} %bitcast.111), channel_id=1, replica_groups=mesh['expert'=32,'dp'=8] {'dp'}, dimensions={0}, use_global_device_ids=true | all-gather | bytes 9216 | tf_op jit(solution)/shard_map/all_gather | solution.py:90
  21.7 4.6 reduce-window.16
  27.1 11.4 %all-gather.1 = bf16[8,32,8]{1,2,0:T(8,128)(2,1)S(1)} all-gather(bf16[1,32,8]{1,2,0:T(8,128)(2,1)} %bitcast.113), channel_id=1, replica_groups=mesh['expert'=32,'dp'=8] {'dp'}, dimensions={0}, use_global_device_ids=true | all-gather | bytes 4608 | tf_op jit(solution)/shard_map/all_gather | solution.py:88
  38.8 1.1 select_reduce_fusion
  39.9 0.7 copy.146
  40.6 11.6 %all-to-all-start = ((bf16[8,32,4]{0,2,1:T(4,128)(2,1)}), bf16[8,32,4]{0,2,1:T(4,128)(2,1)S(1)}, u32[]{:S(2)}, u32[]{:S(2)}) async-start(bf16[8,32,4]{0,2,1:T(4,128)(2,1)} %bitcast.7), calls=%async_computation | async-start | bytes 65536 | tf_op jit(solution)/shard_map/all_to_all | solution.py:117
  52.2 0.7 convert_reduce_fusion
  53.0 7.2 %convolution_convert_fusion = bf16[8,128,4096]{2,1,0:T(8,128)(2,1)} fusion(bf16[8,32,4096]{2,1,0:T(8,128)(2,1)} %bitcast.109, bf16[8,32,128]{2,1,0:T(8,128)(2,1)S(1)} %convert_reduce_fusion), kind=kOutput, calls=%fused_computation.4 | convolution fusion | flops 272629760 | bytes 10551296 | tf_op jit(solution)/shard_map/vmap()/dot_general | solution.py:35
  60.2 13.1 %reshape.326 = bf16[8,32,4,4096]{3,2,1,0:T(4,128)(2,1)} reshape(bf16[8,128,4096]{2,1,0:T(8,128)(2,1)} %convolution_convert_fusion) | data formatting | bytes 16777216 | tf_op jit(solution)/shard_map/reshape | solution.py:104
  73.3 8.5 %copy.137 = bf16[8,32,4,4096]{3,2,0,1:T(4,128)(2,1)} copy(bf16[8,32,4,4096]{3,2,1,0:T(4,128)(2,1)} %reshape.326) | data formatting | bytes 16777216 | tf_op jit(solution)/shard_map/reshape | solution.py:104
  81.7 9.8 %all-to-all-start.2 = ((bf16[8,32,4,4096]{3,2,0,1:T(4,128)(2,1)}), bf16[8,32,4,4096]{3,2,0,1:T(4,128)(2,1)}, u32[]{:S(2)}, u32[]{:S(2)}) async-start(bf16[8,32,4,4096]{3,2,0,1:T(4,128)(2,1)} %copy.137), calls=%async_computation.2 | async-start | bytes 16777216 | tf_op jit(solution)/shard_map/all_to_all | solution.py:103
  91.6 0.7 all-gather.5.cloned.1.call-update
  92.3 30.2 %all-gather.5.cloned.1.call-done = bf16[256,4096]{1,0:T(8,128)(2,1)} async-done(((bf16[32,4096]{1,0:T(8,128)(2,1)}), bf16[256,4096]{1,0:T(8,128)(2,1)}) %all-gather.5.cloned.1.call-update) | async-done | bytes 2097168 | tf_op jit(solution)/shard_map/all_gather | solution.py:87
  122.5 7.2 %convolution_convert_fusion.1 = bf16[8,128,4096]{2,1,0:T(8,128)(2,1)} fusion(bf16[8,32,4096]{2,1,0:T(8,128)(2,1)} %bitcast.110, bf16[8,32,128]{2,1,0:T(8,128)(2,1)S(1)} %convert_reduce_fusion), kind=kOutput, calls=%fused_computation.5 | convolution fusion | flops 272629760 | bytes 10551296 | tf_op jit(solution)/shard_map/vmap()/dot_general | solution.py:38
  129.7 13.1 %reshape.323 = bf16[8,32,4,4096]{3,2,1,0:T(4,128)(2,1)} reshape(bf16[8,128,4096]{2,1,0:T(8,128)(2,1)} %convolution_convert_fusion.1) | data formatting | bytes 16777216 | tf_op jit(solution)/shard_map/reshape | solution.py:111
  142.8 8.5 %copy.135 = bf16[8,32,4,4096]{3,2,0,1:T(4,128)(2,1)} copy(bf16[8,32,4,4096]{3,2,1,0:T(4,128)(2,1)} %reshape.323) | data formatting | bytes 16777216 | tf_op jit(solution)/shard_map/reshape | solution.py:111
  151.2 122.7 %all-to-all-done.2 = bf16[8,32,4,4096]{3,2,0,1:T(4,128)(2,1)} async-done(((bf16[8,32,4,4096]{3,2,0,1:T(4,128)(2,1)}), bf16[8,32,4,4096]{3,2,0,1:T(4,128)(2,1)}, u32[]{:S(2)}, u32[]{:S(2)}) %all-to-all-start.2) | async-done | bytes 8388640 | tf_op jit(solution)/shard_map/all_to_all | solution.py:103
  273.9 21.0 %all-to-all-start.1 = ((bf16[8,32,4,4096]{3,2,0,1:T(4,128)(2,1)}), bf16[8,32,4,4096]{3,2,0,1:T(4,128)(2,1)}, u32[]{:S(2)}, u32[]{:S(2)}) async-start(bf16[8,32,4,4096]{3,2,0,1:T(4,128)(2,1)} %copy.135), calls=%async_computation.1 | async-start | bytes 16777216 | tf_op jit(solution)/shard_map/all_to_all | solution.py:110
  295.0 0.2 reduce-scatter.2.cloned.1.call-start
  295.6 8.5 %copy.138 = bf16[8,32,4,4096]{3,2,1,0:T(4,128)(2,1)} copy(bf16[8,32,4,4096]{3,2,0,1:T(4,128)(2,1)} %all-to-all-done.2) | data formatting | bytes 16777216 | tf_op jit(solution)/shard_map/all_to_all | solution.py:103
  304.1 12.6 %reshape.327 = bf16[1024,4096]{1,0:T(8,128)(2,1)} reshape(bf16[8,32,4,4096]{3,2,1,0:T(4,128)(2,1)} %copy.138) | data formatting | bytes 16777216 | tf_op jit(solution)/shard_map/reshape | solution.py:126
  316.7 7.3 %fusion.18 = f32[192,1024]{1,0:T(8,128)} fusion(bf16[1024,4096]{1,0:T(8,128)(2,1)} %reshape.327, bf16[1,192,4096]{2,1,0:T(8,128)(2,1)S(1)} %copy-done.2), kind=kOutput, calls=%fused_computation.23 | convolution fusion | flops 1610612736 | bytes 10747904 | tf_op jit(solution)/shard_map/dot_general | solution.py:53
  324.0 3.8 fusion.21
  327.8 152.6 %all-to-all-done.1 = bf16[8,32,4,4096]{3,2,0,1:T(4,128)(2,1)} async-done(((bf16[8,32,4,4096]{3,2,0,1:T(4,128)(2,1)}), bf16[8,32,4,4096]{3,2,0,1:T(4,128)(2,1)}, u32[]{:S(2)}, u32[]{:S(2)}) %all-to-all-start.1) | async-done | bytes 8388640 | tf_op jit(solution)/shard_map/all_to_all | solution.py:110
  480.5 8.5 %copy.136 = bf16[8,32,4,4096]{3,2,1,0:T(4,128)(2,1)} copy(bf16[8,32,4,4096]{3,2,0,1:T(4,128)(2,1)} %all-to-all-done.1) | data formatting | bytes 16777216 | tf_op jit(solution)/shard_map/all_to_all | solution.py:110
  488.9 12.5 %reshape.324 = bf16[1024,4096]{1,0:T(8,128)(2,1)} reshape(bf16[8,32,4,4096]{3,2,1,0:T(4,128)(2,1)} %copy.136) | data formatting | bytes 16777216 | tf_op jit(solution)/shard_map/reshape | solution.py:127
  501.5 8.1 %multiply_reduce_fusion = (f32[1024]{0:T(1024)S(1)}, bf16[192,1024]{1,0:T(8,128)(2,1)}, bf16[192,1024]{1,0:T(8,128)(2,1)S(1)}, bf16[192,1024]{1,0:T(8,128)(2,1)S(1)}) fusion(f32[192,1024]{1,0:T(8,128)} %fusion.18, f32[192,1024]{1,0:T(8,128)} %fusion.21, f32[1024]{0:T(1024)S(1)} %reshape.330, bf16[1024,4096]{1,0:T(8,128)(2,1)} %reshape.324, ...), kind=kOutput, calls=%fused_computation.30 | convolution fusion | flops 1614347264 | bytes 12722176 | tf_op jit(solution)/shard_map/dot_general | solution.py:56
  509.6 8.1 %fusion.6 = f32[1024,4096]{1,0:T(8,128)} fusion(bf16[192,1024]{1,0:T(8,128)(2,1)S(1)} %get-tuple-element.7, bf16[1,192,4096]{2,1,0:T(8,128)(2,1)S(1)} %copy-done), kind=kOutput, calls=%fused_computation.13 | convolution fusion | flops 1610612736 | bytes 18743296 | tf_op jit(solution)/shard_map/dot_general | solution.py:132
  517.7 11.3 %add_convert_fusion = bf16[1024,4096]{1,0:T(8,128)(2,1)} fusion(f32[1024,4096]{1,0:T(8,128)} %fusion.6, bf16[192,1024]{1,0:T(8,128)(2,1)S(1)} %get-tuple-element.8, bf16[1,192,4096]{2,1,0:T(8,128)(2,1)S(1)} %copy-done.2), kind=kOutput, calls=%fused_computation.1 | convolution fusion | flops 1619001344 | bytes 27131904 | tf_op jit(solution)/shard_map/dot_general | solution.py:138
  529.1 0.7 copy-done.5
  530.0 0.6 reduce-window.14
  530.6 0.2 slice_reduce_fusion
  531.1 0.6 dynamic-slice
  532.4 14.1 %all-reduce = bf16[1024]{0:T(1024)(128)(2,1)S(1)} all-reduce(f32[1024]{0:T(1024)S(1)} %get-tuple-element.5), channel_id=3, replica_groups=mesh['expert'=32,'dp'=8] {'dp'}, use_global_device_ids=true, to_apply=%region_10.11.clone | all-reduce | flops 1024 | bytes 6144
  546.6 0.7 convert_element_type.129
  547.3 17.0 %all-to-all-start.4 = ((bf16[32,1,4]{2,1,0:T(2,128)(2,1)}), bf16[32,1,4]{2,1,0:T(2,128)(2,1)S(1)}, u32[]{:S(2)}, u32[]{:S(2)}) async-start(bf16[32,1,4]{2,1,0:T(2,128)(2,1)} %convert_element_type.129), calls=%async_computation.5 | async-start | bytes 32768 | tf_op jit(solution)/shard_map/all_to_all | solution.py:155
  564.5 27.8 %reduce-scatter.2.cloned.1.call-done = bf16[128,4096]{1,0:T(8,128)(2,1)} async-done(((bf16[1024,4096]{1,0:T(8,128)(2,1)}), bf16[128,4096]{1,0:T(8,128)(2,1)}) %reduce-scatter.2.cloned.1.call-update) | async-done | bytes 1048592 | tf_op jit(solution)/shard_map/reduce_scatter | solution.py:135
  592.3 2.3 convert_element_type.117
  594.6 10.1 %all-to-all-start.3 = ((bf16[32,4,4096]{2,1,0:T(4,128)(2,1)}), bf16[32,4,4096]{2,1,0:T(4,128)(2,1)S(1)}, u32[]{:S(2)}, u32[]{:S(2)}) async-start(bf16[32,4,4096]{2,1,0:T(4,128)(2,1)} %convert_element_type.117), calls=%async_computation.4 | async-start | bytes 2097152 | tf_op jit(solution)/shard_map/all_to_all | solution.py:148
  604.7 6.5 %fusion.4 = bf16[1,192,4096]{2,1,0:T(8,128)(2,1)} fusion(bf16[192,1024]{1,0:T(8,128)(2,1)S(1)} %copy-done.4, bf16[1024,4096]{1,0:T(8,128)(2,1)} %reshape.327), kind=kOutput, calls=%fused_computation.10 | convolution fusion | flops 1611399168 | bytes 10354688 | tf_op jit(solution)/shard_map/dot_general | solution.py:72
  611.2 6.5 %fusion.3 = bf16[1,192,4096]{2,1,0:T(8,128)(2,1)} fusion(bf16[192,1024]{1,0:T(8,128)(2,1)S(1)} %get-tuple-element.7, bf16[1024,4096]{1,0:T(8,128)(2,1)} %reshape.327), kind=kOutput, calls=%fused_computation.9 | convolution fusion | flops 1611399168 | bytes 10354688 | tf_op jit(solution)/shard_map/dot_general | solution.py:71
  617.7 3.3 fusion.5
  621.1 0.5 fusion.40
  621.6 0.7 copy.147
  622.3 10.0 %all-to-all-done.3 = bf16[32,4,4096]{2,1,0:T(4,128)(2,1)S(1)} async-done(((bf16[32,4,4096]{2,1,0:T(4,128)(2,1)}), bf16[32,4,4096]{2,1,0:T(4,128)(2,1)S(1)}, u32[]{:S(2)}, u32[]{:S(2)}) %all-to-all-start.3) | async-done | bytes 1048608 | tf_op jit(solution)/shard_map/all_to_all | solution.py:148
  632.3 1.1 reshape.328
  633.4 2.5 convolution_convert_fusion.4
  (66 shorter events, 2.7 us)
Async XLA Ops:
  7.2 316.9 %copy-start = (bf16[1,192,4096]{2,1,0:T(8,128)(2,1)S(1)}, bf16[1,192,4096]{2,1,0:T(8,128)(2,1)}, u32[]{:S(2)}) copy-start(bf16[1,192,4096]{2,1,0:T(8,128)(2,1)} %param.11) | copy-start | bytes 4718596
  7.2 45.8 %all-gather.7.cloned.1.call-start = ((), (), s32[]{:S(2)}) async-start(), calls=%async_computation.7 | async-start | bytes 2359296 | tf_op jit(solution)/shard_map/all_gather | solution.py:86
  40.6 41.1 %all-to-all-start = ((bf16[8,32,4]{0,2,1:T(4,128)(2,1)}), bf16[8,32,4]{0,2,1:T(4,128)(2,1)S(1)}, u32[]{:S(2)}, u32[]{:S(2)}) async-start(bf16[8,32,4]{0,2,1:T(4,128)(2,1)} %bitcast.7), calls=%async_computation | async-start | bytes 65536 | tf_op jit(solution)/shard_map/all_to_all | solution.py:117
  81.7 192.2 %all-to-all-start.2 = ((bf16[8,32,4,4096]{3,2,0,1:T(4,128)(2,1)}), bf16[8,32,4,4096]{3,2,0,1:T(4,128)(2,1)}, u32[]{:S(2)}, u32[]{:S(2)}) async-start(bf16[8,32,4,4096]{3,2,0,1:T(4,128)(2,1)} %copy.137), calls=%async_computation.2 | async-start | bytes 16777216 | tf_op jit(solution)/shard_map/all_to_all | solution.py:103
  91.6 30.9 %all-gather.5.cloned.1.call-start = ((), (), s32[]{:S(2)}) async-start(), calls=%async_computation.6 | async-start | bytes 2359296 | tf_op jit(solution)/shard_map/all_gather | solution.py:87
  273.9 206.5 %all-to-all-start.1 = ((bf16[8,32,4,4096]{3,2,0,1:T(4,128)(2,1)}), bf16[8,32,4,4096]{3,2,0,1:T(4,128)(2,1)}, u32[]{:S(2)}, u32[]{:S(2)}) async-start(bf16[8,32,4,4096]{3,2,0,1:T(4,128)(2,1)} %copy.135), calls=%async_computation.1 | async-start | bytes 16777216 | tf_op jit(solution)/shard_map/all_to_all | solution.py:110
  295.0 297.3 %reduce-scatter.2.cloned.1.call-start = ((), (), s32[]{:S(2)}) async-start(), calls=%async_computation.8 | async-start | bytes 9437184 | tf_op jit(solution)/shard_map/reduce_scatter | solution.py:135
  304.1 12.7 %copy-start.2 = (bf16[1,192,4096]{2,1,0:T(8,128)(2,1)S(1)}, bf16[1,192,4096]{2,1,0:T(8,128)(2,1)}, u32[]{:S(2)}) copy-start(bf16[1,192,4096]{2,1,0:T(8,128)(2,1)} %param.12) | copy-start | bytes 4718596
  316.7 7.3 %copy-start.1 = (bf16[1024,4096]{1,0:T(8,128)(2,1)S(1)}, bf16[1024,4096]{1,0:T(8,128)(2,1)}, u32[]{:S(2)}) copy-start(bf16[1024,4096]{1,0:T(8,128)(2,1)} %reshape.327) | copy-start | bytes 25165828
  509.6 8.1 %copy-start.3 = (bf16[192,1024]{1,0:T(8,128)(2,1)}, bf16[192,1024]{1,0:T(8,128)(2,1)S(1)}, u32[]{:S(2)}) copy-start(bf16[192,1024]{1,0:T(8,128)(2,1)S(1)} %get-tuple-element.8) | copy-start | bytes 1179652
  529.1 0.7 copy-start.5
  529.1 2.0 copy-start.6
  529.1 75.6 %copy-start.4 = (bf16[192,1024]{1,0:T(8,128)(2,1)S(1)}, bf16[192,1024]{1,0:T(8,128)(2,1)}, u32[]{:S(2)}) copy-start(bf16[192,1024]{1,0:T(8,128)(2,1)} %copy-done.3) | copy-start | bytes 1179652
  547.3 47.3 %all-to-all-start.4 = ((bf16[32,1,4]{2,1,0:T(2,128)(2,1)}), bf16[32,1,4]{2,1,0:T(2,128)(2,1)S(1)}, u32[]{:S(2)}, u32[]{:S(2)}) async-start(bf16[32,1,4]{2,1,0:T(2,128)(2,1)} %convert_element_type.129), calls=%async_computation.5 | async-start | bytes 32768 | tf_op jit(solution)/shard_map/all_to_all | solution.py:155
  594.6 37.7 %all-to-all-start.3 = ((bf16[32,4,4096]{2,1,0:T(4,128)(2,1)}), bf16[32,4,4096]{2,1,0:T(4,128)(2,1)S(1)}, u32[]{:S(2)}, u32[]{:S(2)}) async-start(bf16[32,4,4096]{2,1,0:T(4,128)(2,1)} %convert_element_type.117), calls=%async_computation.4 | async-start | bytes 2097152 | tf_op jit(solution)/shard_map/all_to_all | solution.py:148
  604.7 13.0 %slice-start = ((s8[8388608]{0:T(1024)(128)(4,1)}), s8[4194304]{0:T(1024)(128)(4,1)S(1)}, s32[]{:S(2)}) async-start(s8[8388608]{0:T(1024)(128)(4,1)} %bitcast.107), calls=%async_computation.9 | async-start | bytes 8388608
  611.2 6.5 %slice-start.1 = ((s8[8388608]{0:T(1024)(128)(4,1)}), s8[4194304]{0:T(1024)(128)(4,1)S(1)}, s32[]{:S(2)}) async-start(s8[8388608]{0:T(1024)(128)(4,1)} %bitcast.107), calls=%async_computation.10 | async-start | bytes 8388608
  611.2 6.5 %copy-start.7 = (bf16[192,1024]{1,0:T(8,128)(2,1)S(1)}, bf16[192,1024]{1,0:T(8,128)(2,1)}, u32[]{:S(2)}) copy-start(bf16[192,1024]{1,0:T(8,128)(2,1)} %get-tuple-element.6) | copy-start | bytes 1179652
Sparse Core Ops, SparseCore 0:
  9.8 30.5 all-gather.6
  94.2 28.2 all-gather.4
  529.2 63.0 reduce-scatter.1
where the time goes:
time: 645 us; the launch traced here: 642 us
  waiting for transfers between devices  345 us (53%)
  local copies, waits for them, and re-layouts  93.9 us (15%)
  matrix products  72.2 us (11%)
  starting transfers between devices  69.9 us (11%)
  blocking collectives  38.9 us (6%)
  between operations  14.7 us (2%)
  other arithmetic  7.98 us (1%)
    all_to_all x1, waiting for transfers between devices, body(): lax.all_to_all(outgoing[1].reshape(n_members, n_targets, CAP, model_width...  153 us
    all_to_all x1, waiting for transfers between devices, body(): lax.all_to_all(outgoing[0].reshape(n_members, n_targets, CAP, model_width...  123 us
    all_gather x1, waiting for transfers between devices, body(): lax.all_gather(out_grad, 'dp', axis=0, tiled=True)  30.2 us
    reduce_scatter x1, waiting for transfers between devices, body(): lax.psum_scatter((term + lax.dot_general(up_pre_all, weights[1], CONTRACT...  27.8 us
    reshape x2, local copies, waits for them, and re-layouts, body(): outgoing[0].reshape(n_members, n_targets, CAP, model_width)  21.5 us
    reshape x2, local copies, waits for them, and re-layouts, body(): outgoing[1].reshape(n_members, n_targets, CAP, model_width)  21.5 us
    all_to_all x1, starting transfers between devices, body(): lax.all_to_all(outgoing[1].reshape(n_members, n_targets, CAP, model_width...  21 us
    all_to_all x1, starting transfers between devices, body(): lax.all_to_all(slot_gates.reshape(n_targets, CAP).astype(jnp.bfloat16), '...  17 us
  transfers between devices with their start and end apart: 8, of which 5 were waited for; matrix products, arithmetic and copies ran while one was open for 19% of the time, Pallas kernels for 0%

commit v1 on v0

v1 whole, which is shorter than its diff:
```python
import jax
import jax.numpy as jnp
from jax import lax
from jax.experimental import pallas as pl
from jax.experimental.pallas import tpu as pltpu
from jax.sharding import PartitionSpec as P

EXPERTS = 128
CAP = 4
NX = 4
NC = 2
NY = 4
CHUNKS = 8
LANES = 128
MESH = pl.DeviceIdType.MESH
LAST = (((1,), (1,)), ((), ()))
F32 = jnp.float32
BF16 = jnp.bfloat16


def mm(a, b):
    return jnp.dot(a, b, preferred_element_type=F32)


def mm_t(a, b):
    return lax.dot_general(a, b, LAST, preferred_element_type=F32)


def rows_of(index, size):
    return pl.ds(pl.multiple_of(index * size, size), size)


def kernel(
    nz, tok, og, pp, wg, wu, wd,
    tg_out, ext_out, gg_out, gu_out, gd_out,
    pb, pm, pgm, ptm, ty, zs, xg, ww, acc, gp, up, hd, gpt, upt, hdt,
    ps, pk, pr, hl, hr, fl, fr, rs, rz, ts, tr, go,
    pse, pke, pre, hle, hre, fle, fre, rse, rze, tse, tre,
    s_p, s_y, s_z, s_xl, s_xr, s_fl, s_fr, s_c, s_w,
    t_p, t_y, t_z, t_x,
    r_c, r_hl, r_hr, r_fl, r_fr, r_z, r_y,
    u_c, u_h, u_f, u_z, u_y, u_o,
):
    chunks, _, block_tokens, width = ty.shape
    toks = block_tokens // NY
    unit = NY * CAP
    block = nz * unit
    half = block // 2
    column = NX * block
    e = lax.axis_index("expert")
    m = lax.axis_index("dp")
    z, y = e // NY, lax.rem(e, NY)
    x, core = m // NC, lax.rem(m, NC)
    other = 1 - core
    xr, xl, xo = lax.rem(x + 1, NX), lax.rem(x + NX - 1, NX), lax.rem(x + 2, NX)
    right, left, partner = (e, xr * NC + core), (e, xl * NC + core), (e, x * NC + other)
    y_peers = [lax.rem(y + d, NY) for d in range(1, NY)]
    z_peers = [lax.rem(z + d, nz) for d in range(1, nz)]

    def at_y(v):
        return (z * NY + v, m)

    def at_z(v):
        return (v * NY + y, m)

    def send(src, dst, ssem, rsem, dev):
        pltpu.make_async_remote_copy(
            src_ref=src, dst_ref=dst, send_sem=ssem, recv_sem=rsem,
            device_id=dev, device_id_type=MESH,
        ).start()

    def local(src, dst, sem):
        pltpu.make_async_copy(src, dst, sem).start()

    def take(ref, sem):
        pltpu.make_async_copy(ref, ref, sem).wait()

    barrier = pltpu.get_barrier_semaphore()
    peers = [at_y(v) for v in y_peers] + [at_z(v) for v in z_peers] + [right, left, partner]
    for dev in peers:
        pl.semaphore_signal(barrier, inc=1, device_id=dev, device_id_type=MESH)
    pl.semaphore_wait(barrier, len(peers))

    for v in y_peers:
        send(pp.at[v], pb.at[y], t_p, s_p, at_y(v))
    local(pp.at[y], pb.at[y], s_p)

    @pl.loop(0, chunks)
    def _(c):
        cols = rows_of(c, width)
        mine = rows_of(y, toks)
        for a, src in enumerate((tok, og)):
            for v in y_peers:
                send(src.at[:, cols], ty.at[c, a, mine], t_y.at[c], s_y.at[c], at_y(v))
            local(src.at[:, cols], ty.at[c, a, mine], s_y.at[c])

    @pl.loop(0, chunks)
    def _(c):
        cols = rows_of(c, width)
        for i, src in enumerate((wg, wu, wd)):
            local(src.at[:, cols], ww.at[c, i], s_w)

    take(pb, s_p)
    total = pb[0].astype(F32)
    for v in range(1, NY):
        total = total + pb[v].astype(F32)
    pm[...] = total[0].astype(BF16)
    pgm[...] = total[1].astype(BF16)
    ptm[...] = total[0].T.astype(BF16)
    acc[...] = jnp.zeros_like(acc)

    mine_rows = rows_of(core * NX + x, block)
    left_rows = rows_of(core * NX + xl, block)
    right_rows = rows_of(core * NX + xr, block)
    opp_rows = rows_of(core * NX + xo, block)
    opp_0 = rows_of((core * NX + xo) * 2, half)
    opp_1 = rows_of((core * NX + xo) * 2 + 1, half)
    left_0 = rows_of((core * NX + xl) * 2, half)
    right_1 = rows_of((core * NX + xr) * 2 + 1, half)
    my_unit = rows_of(z, unit)

    def stage_z(c):
        take(ty.at[c], s_y.at[c])
        zs[c, 0] = mm(pm[...], ty[c, 0]).astype(BF16)
        zs[c, 1] = mm(pgm[...], ty[c, 1]).astype(BF16)
        dst = xg.at[c, :, rows_of((core * NX + x) * nz + z, unit)]
        for v in z_peers:
            send(zs.at[c, :, rows_of(v, unit)], dst, t_z.at[c], s_z.at[c], at_z(v))
        local(zs.at[c, :, my_unit], dst, s_z.at[c])

    def stage_x(c):
        own = xg.at[c, :, mine_rows]
        take(own, s_z.at[c])
        send(own, own, t_x.at[c], s_xl.at[c], right)
        send(own, own, t_x.at[c], s_xr.at[c], left)
        send(own, own, t_x.at[c], s_c.at[c], partner)

    def stage_x2(c):
        from_left = xg.at[c, :, left_rows]
        take(from_left, s_xl.at[c])
        part = xg.at[c, :, left_0]
        send(part, part, t_x.at[c], s_fl.at[c], right)
        send(from_left, from_left, t_x.at[c], s_c.at[c], partner)
        from_right = xg.at[c, :, right_rows]
        take(from_right, s_xr.at[c])
        part = xg.at[c, :, right_1]
        send(part, part, t_x.at[c], s_fr.at[c], left)
        send(from_right, from_right, t_x.at[c], s_c.at[c], partner)

    def stage_x3(c):
        take(xg.at[c, :, opp_0], s_fl.at[c])
        take(xg.at[c, :, opp_1], s_fr.at[c])
        opp = xg.at[c, :, opp_rows]
        send(opp, opp, t_x.at[c], s_c.at[c], partner)

    def stage_f(c):
        @pl.when(c == 0)
        def _():
            take(ww, s_w)

        take(xg.at[c, :, rows_of(other, column)], s_c.at[c])

        @pl.loop(0, NC * NX // 2)
        def _(b):
            rows = rows_of(b, 2 * block)
            xs = xg[c, 0, rows]
            acc[0, rows] += mm_t(xs, ww[c, 0])
            acc[1, rows] += mm_t(xs, ww[c, 1])
            acc[2, rows] += mm_t(xg[c, 1, rows], ww[c, 2])

    stages = (stage_z, stage_x, stage_x2, stage_x3, stage_f)

    @pl.loop(0, chunks + len(stages) - 1)
    def _(t):
        for lag, stage in enumerate(stages):
            c = t - lag

            @pl.when(jnp.logical_and(c >= 0, c < chunks))
            def _(stage=stage, c=c):
                stage(c)

    def activate(rows):
        pre_gate, pre_up, hidden_grad = acc[0, rows], acc[1, rows], acc[2, rows]
        squash = jax.nn.sigmoid(pre_gate)
        activated = pre_gate * squash
        hidden = (activated * pre_up).astype(BF16)
        terms = jnp.sum(hidden.astype(F32) * hidden_grad, axis=1, keepdims=True)
        up_grad = hidden_grad * activated
        gate_grad = hidden_grad * pre_up * squash * (1.0 + pre_gate * (1.0 - squash))
        gp[rows] = gate_grad.astype(BF16)
        up[rows] = up_grad.astype(BF16)
        hd[rows] = hidden
        lane = lax.broadcasted_iota(jnp.int32, (block, LANES), 1)
        return jnp.where(lane == e, terms, 0.0).astype(BF16)

    @pl.loop(0, NX)
    def _(b):
        pse[rows_of(b, block)] = activate(rows_of(other * NX + b, block))
        pke[rows_of(b, block)] = activate(rows_of(core * NX + b, block))

    main = (ps, pk, pr, hl, hr, fl, fr, rs, rz, ts, tr)
    extra = (pse, pke, pre, hle, hre, fle, fre, rse, rze, tse, tre)

    def pick(refs, c):
        return [r.at[c] for r in refs] if refs is main else list(refs)

    def to_partner(refs, c):
        b = pick(refs, c)
        send(b[0], b[2], u_c.at[c], r_c.at[c], partner)

    def stage_pair(c):
        rows = rows_of(other, column)
        ps[c] = (mm(gp[rows], ww[c, 0]) + mm(up[rows], ww[c, 1])).astype(BF16)
        to_partner(main, c)
        rows = rows_of(core, column)
        pk[c] = (mm(gp[rows], ww[c, 0]) + mm(up[rows], ww[c, 1])).astype(BF16)

    def stage_r1(refs, c):
        _, keep, came, to_l, to_r, *_ = pick(refs, c)
        take(came, r_c.at[c])

        @pl.loop(0, NX)
        def _(b):
            rows = rows_of(b, block)
            keep[rows] = (keep[rows].astype(F32) + came[rows].astype(F32)).astype(BF16)

        send(keep.at[rows_of(xo * 2, half)], to_l, u_h.at[c], r_hl.at[c], right)
        send(keep.at[rows_of(xo * 2 + 1, half)], to_r, u_h.at[c], r_hr.at[c], left)

    def stage_r2(refs, c):
        _, keep, _, half_l, half_r, full_l, full_r, *_ = pick(refs, c)
        take(half_l, r_hl.at[c])
        rows = rows_of(xr * 2, half)
        keep[rows] = (keep[rows].astype(F32) + half_l[...].astype(F32)).astype(BF16)
        send(keep.at[rows_of(xr, block)], full_l, u_f.at[c], r_fl.at[c], right)
        take(half_r, r_hr.at[c])
        rows = rows_of(xl * 2 + 1, half)
        keep[rows] = (keep[rows].astype(F32) + half_r[...].astype(F32)).astype(BF16)
        send(keep.at[rows_of(xl, block)], full_r, u_f.at[c], r_fr.at[c], left)

    def stage_r3(refs, c):
        _, keep, _, _, _, full_l, full_r, done, back, *_ = pick(refs, c)
        take(full_l, r_fl.at[c])
        take(full_r, r_fr.at[c])
        done[...] = (
            keep[rows_of(x, block)].astype(F32)
            + full_l[...].astype(F32)
            + full_r[...].astype(F32)
        ).astype(BF16)
        for v in z_peers:
            send(done.at[rows_of(v, unit)], back.at[my_unit], u_z.at[c], r_z.at[c], at_z(v))
        local(done.at[my_unit], back.at[my_unit], r_z.at[c])

    def stage_r4(refs, c):
        *_, back, parts, summed = pick(refs, c)
        take(back, r_z.at[c])
        parts[...] = mm(ptm[...], back[...]).astype(BF16)
        mine = rows_of(y, toks)
        for v in y_peers:
            send(parts.at[rows_of(v, toks)], summed.at[mine], u_y.at[c], r_y.at[c], at_y(v))
        local(parts.at[mine], summed.at[mine], r_y.at[c])

    def stage_r5(refs, c):
        summed = pick(refs, c)[-1]
        take(summed, r_y.at[c])
        out = summed[pl.ds(0, toks)].astype(F32)
        for v in range(1, NY):
            out = out + summed[pl.ds(v * toks, toks)].astype(F32)
        if refs is main:
            tg_out[:, rows_of(c, width)] = out.astype(BF16)
        else:
            ext_out[...] = out

    def transposes():
        for src, dst in ((gp, gpt), (up, upt), (hd, hdt)):
            @pl.loop(0, NC * NX)
            def _(b, src=src, dst=dst):
                rows = rows_of(b, block)
                dst[:, rows] = src[rows].astype(F32).T.astype(BF16)

    def weight_grads(c):
        cols = rows_of(c, width)
        tokens_c = xg[c, 0]
        go[c, 0] = mm(gpt[...], tokens_c).astype(BF16)
        go[c, 1] = mm(upt[...], tokens_c).astype(BF16)
        go[c, 2] = mm(hdt[...], xg[c, 1]).astype(BF16)
        for i, dst in enumerate((gg_out, gu_out, gd_out)):
            local(go.at[c, i], dst.at[0, :, cols], u_o.at[c, i])

    to_partner(extra, chunks)
    returns = (stage_r1, stage_r2, stage_r3, stage_r4, stage_r5)

    @pl.loop(0, chunks + len(returns))
    def _(t):
        @pl.when(t < chunks)
        def _():
            stage_pair(t)

        for lag, stage in enumerate(returns):
            @pl.when(t == lag)
            def _(stage=stage):
                stage(extra, chunks)

            c = t - lag - 1

            @pl.when(jnp.logical_and(c >= 0, c < chunks))
            def _(stage=stage, c=c):
                stage(main, c)

        @pl.when(t == 0)
        def _():
            transposes()

        @pl.when(t < chunks)
        def _():
            weight_grads(t)

    take(pb.at[pl.ds(1, NY - 1)], t_p)

    def drain(refs, c):
        b = pick(refs, c)
        take(b[0], u_c.at[c])
        take(b[5], u_h.at[c])
        take(b[1].at[pl.ds(0, 2 * block)], u_f.at[c])
        take(b[8].at[pl.ds(0, block - unit)], u_z.at[c])
        take(b[10].at[pl.ds(0, block_tokens - toks)], u_y.at[c])

    drain(extra, chunks)

    @pl.loop(0, chunks)
    def _(c):
        take(ty.at[c, :, pl.ds(0, block_tokens - toks)], t_y.at[c])
        take(zs.at[c, :, pl.ds(0, block - unit)], t_z.at[c])
        take(xg.at[c, :, pl.ds(0, 7 * block)], t_x.at[c])
        drain(main, c)
        cols = rows_of(c, width)
        for i, dst in enumerate((gg_out, gu_out, gd_out)):
            pltpu.make_async_copy(go.at[c, i], dst.at[0, :, cols], u_o.at[c, i]).wait()


def run(tokens, out_grad, pp, w_gate, w_up, w_down, nz):
    toks, depth = tokens.shape
    units = w_gate.shape[0]
    chunks = CHUNKS
    width = depth // chunks
    block = nz * NY * CAP
    total = block * NX * NC
    column = block * NX
    any_spec = pl.BlockSpec(memory_space=pl.ANY)
    vmem_spec = pl.BlockSpec(memory_space=pltpu.VMEM)
    dma = pltpu.SemaphoreType.DMA
    v = pltpu.VMEM

    def back(lead, w):
        return [
            v(lead + (column, w), BF16),
            v(lead + (column, w), BF16),
            v(lead + (column, w), BF16),
            v(lead + (block // 2, w), BF16),
            v(lead + (block // 2, w), BF16),
            v(lead + (block, w), BF16),
            v(lead + (block, w), BF16),
            v(lead + (block, w), BF16),
            v(lead + (block, w), BF16),
            v(lead + (NY * toks, w), BF16),
            v(lead + (NY * toks, w), BF16),
        ]

    scratch = [
        v((NY, 2, block, NY * toks), BF16),
        v((block, NY * toks), BF16),
        v((block, NY * toks), BF16),
        v((NY * toks, block), BF16),
        v((chunks, 2, NY * toks, width), BF16),
        v((chunks, 2, block, width), BF16),
        v((chunks, 2, total, width), BF16),
        v((chunks, 3, units, width), BF16),
        v((3, total, units), F32),
        v((total, units), BF16),
        v((total, units), BF16),
        v((total, units), BF16),
        v((units, total), BF16),
        v((units, total), BF16),
        v((units, total), BF16),
        *back((chunks,), width),
        v((chunks, 3, units, width), BF16),
        *back((), LANES),
        dma(()), *[dma((chunks,)) for _ in range(7)], dma(()),
        dma(()), *[dma((chunks,)) for _ in range(3)],
        *[dma((chunks + 1,)) for _ in range(7)],
        *[dma((chunks + 1,)) for _ in range(5)],
        dma((chunks, 3)),
    ]
    grads = jax.ShapeDtypeStruct((1, units, depth), BF16)

    def body(*refs):
        kernel(nz, *refs)

    return pl.pallas_call(
        body,
        out_shape=(
            jax.ShapeDtypeStruct((toks, depth), BF16),
            jax.ShapeDtypeStruct((toks, LANES), F32),
            grads, grads, grads,
        ),
        in_specs=[any_spec] * 6,
        out_specs=(vmem_spec, vmem_spec, any_spec, any_spec, any_spec),
        scratch_shapes=scratch,
        compiler_params=pltpu.CompilerParams(
            collective_id=0, has_side_effects=True, vmem_limit_bytes=67043328
        ),
    )(tokens, out_grad, pp, w_gate, w_up, w_down)


def body(tokens, out_grad, gate_probs, route_ids, w_gate, w_up, w_down):
    n_targets = lax.axis_size("expert")
    nz = n_targets // NY
    toks = tokens.shape[0]
    per_device = EXPERTS // n_targets
    y = lax.rem(lax.axis_index("expert"), NY)
    gates = gate_probs.astype(F32)
    named = route_ids[:, :, None] == per_device * jnp.arange(n_targets, dtype=jnp.int32)
    active = jnp.any(named, axis=1).astype(F32)
    weight = jnp.sum(jnp.where(named, gates[:, :, None], 0.0), axis=1)
    order = jnp.arange(toks)
    before = (order[:, None] > order[None, :]).astype(F32)
    rank = jnp.dot(before, active, preferred_element_type=F32)
    placed = jnp.logical_and(
        active.T[:, None, :] > 0.0,
        rank.T[:, None, :] == jnp.arange(CAP, dtype=F32)[None, :, None],
    )
    one = placed.astype(F32)
    scaled = jnp.where(placed, weight.T[:, None, :], 0.0)
    both = jnp.stack([one, scaled]).reshape(2, nz, NY, CAP, toks)
    mine = (jnp.arange(NY) == y).astype(F32)
    spread = (
        both.transpose(2, 0, 1, 3, 4)[:, :, :, None, :, None, :]
        * mine[None, None, None, :, None, None, None]
        * mine[None, None, None, None, None, :, None]
    )
    pp = spread.reshape(NY, 2, nz * NY * CAP, NY * toks).astype(BF16)
    token_grad, ext, grad_gate, grad_up, grad_down = run(
        tokens, out_grad, pp, w_gate[0], w_up[0], w_down[0], nz
    )
    values = jnp.sum(jnp.where(named, ext[:, None, :n_targets], 0.0), axis=2)
    return token_grad, values / gates, grad_gate, grad_up, grad_down


def solution(mesh):
    in_specs = (
        P(("expert", "dp"), None),
        P(("expert", "dp"), None),
        P(("expert", "dp"), None),
        P(("expert", "dp"), None),
        P("expert", "dp", None),
        P("expert", "dp", None),
        P("expert", "dp", None),
    )
    out_specs = (
        P(("expert", "dp"), None),
        P(("expert", "dp"), None),
        P("expert", "dp", None),
        P("expert", "dp", None),
        P("expert", "dp", None),
    )
    return jax.shard_map(body, mesh=mesh, in_specs=in_specs, out_specs=out_specs, check_vma=False)
```

time: 645 us -> 174 us (0.27)
  waiting for transfers between devices: 345 us -> 0 us
  Pallas kernels: 0 us -> 158 us
  local copies, waits for them, and re-layouts: 93.9 us -> 11.7 us
  matrix products: 72.2 us -> 0.13 us
  starting transfers between devices: 69.9 us -> 0 us
  blocking collectives: 38.9 us -> 0 us
  between operations: 14.7 us -> 0.77 us
    all_to_all x5 -> x0, waiting for transfers between devices: 285 us -> none  [the longest x1 153 us: body(): lax.all_to_all(outgoing[1].reshape(n_members, n_targets, CAP, model_width...]
    pallas_call x0 -> x1, Pallas kernels: none -> 158 us  [run(): pl.pallas_call(body, out_shape=(jax.ShapeDtypeStruct((toks, depth), BF16)...]
    dot_general x12 -> x1, matrix products: 72.2 us -> 0.13 us  [body(): rank = jnp.dot(before, active, preferred_element_type=F32)]
    reshape x10 -> x0, local copies, waits for them, and re-layouts: 69.6 us -> none  [the longest x2 21.5 us: body(): outgoing[0].reshape(n_members, n_targets, CAP, model_width)]
    all_to_all x5 -> x0, starting transfers between devices: 69.6 us -> none  [the longest x1 21 us: body(): lax.all_to_all(outgoing[1].reshape(n_members, n_targets, CAP, model_width...]
    all_gather x2 -> x0, waiting for transfers between devices: 30.2 us -> none  [the longest x1 30.2 us: body(): lax.all_gather(out_grad, 'dp', axis=0, tiled=True)]
    reduce_scatter x1 -> x0, waiting for transfers between devices: 27.8 us -> none  [body(): lax.psum_scatter((term + lax.dot_general(up_pre_all, weights[1], CONTRACT...]
    all_gather x2 -> x0, blocking collectives: 24.8 us -> none  [the longest x1 13.4 us: body(): group_ids = lax.all_gather(route_ids, 'dp', axis=0, tiled=True)]
  transfers between devices with their start and end apart: 8 -> 0, of which waited for: 5 -> 0; matrix products, arithmetic and copies ran while one was open for 19% -> 0% of each run, Pallas kernels for 0% -> 0%
where the time goes in v1:
time: 174 us; the launch traced here: 173 us
  Pallas kernels  158 us (91%)
  local copies, waits for them, and re-layouts  11.7 us (7%)
  other arithmetic  2.94 us (2%)
    pallas_call x1, Pallas kernels, run(): pl.pallas_call(body, out_shape=(jax.ShapeDtypeStruct((toks, depth), BF16)...  158 us
    unnamed x17, local copies, waits for them, and re-layouts  9.82 us

profile of v1, /device:TPU:16, one launch (start us, length us, event | category | flops | bytes accessed | tf_op | source)
XLA Modules:
  0.0 173.1 jit_solution(5761987573108780157)
XLA Ops:
  0.7 0.0 copy-start.4
  0.7 0.1 mul.55
  0.7 0.1 mul.56
  0.8 0.8 copy.24
  1.6 0.0 copy-start.3
  1.6 0.8 copy.19
  2.4 0.0 copy-start.2
  2.4 0.1 compare_reduce_fusion
  2.5 0.1 copy.22
  2.6 0.1 copy.20
  2.7 0.1 fusion.6
  2.8 0.2 fusion
  3.0 0.0 copy-done.4
  3.0 0.1 copy.25
  3.2 0.0 copy-done.3
  3.2 0.0 copy-done.2
  3.2 0.2 broadcast_multiply_fusion
  3.4 0.6 mul.53
  4.0 0.9 mul.54
  4.8 0.8 multiply_convert_fusion.refs_2_
  5.6 157.6 %shard_map.110 = (bf16[32,4096]{1,0:T(8,128)(2,1)}, f32[32,128]{1,0:T(8,128)}, bf16[1,192,4096]{2,1,0:T(8,128)(2,1)}, bf16[1,192,4096]{2,1,0:T(8,128)(2,1)}, bf16[1,192,4096]{2,1,0:T(8,128)(2,1)}) custom-call(bf16[32,4096]{1,0:T(8,128)(2,1)} %refs_0_.1, bf16[32,4096]{1,0:T(8,128)(2,1)} %refs_1_.1, bf16[4,2,128,128]{3,2,1,0:T(8,128)(2,1)} %multiply_convert_fusion.refs_2_, ...), custom_call_target="tpu_custom_call" | custom-call | tf_op jit(solution)/shard_map/pallas_call | solution.py:399
  163.2 0.9 fusion.1
  164.1 0.7 convert_divide_fusion
  164.9 0.7 copy.27
  165.5 1.7 copy.34
  167.2 0.0 copy-start.1
  167.2 2.8 %copy.35 = bf16[1,192,4096]{2,1,0:T(8,128)(2,1)} copy(bf16[1,192,4096]{2,1,0:T(8,128)(2,1)} %get-tuple-element.27) | data formatting | bytes 3145728
  170.0 0.0 copy-done.1
  170.0 0.0 copy-start
  170.0 1.1 copy.36
  171.2 0.8 copy-done
  172.0 1.1 copy.37
  (9 shorter events, 0.1 us)
Async XLA Ops:
  0.7 2.3 %copy-start.4 = (s32[32]{0:T(128)}, s32[32]{0:T(128)S(1)}, u32[]{:S(2)}) copy-start(s32[32]{0:T(128)S(1)} %iota_multiply_fusion) | copy-start | bytes 388
  1.6 1.6 copy-start.3
  2.4 0.9 copy-start.2
  167.2 2.8 %copy-start.1 = (bf16[1,192,4096]{2,1,0:T(8,128)(2,1)S(1)}, bf16[1,192,4096]{2,1,0:T(8,128)(2,1)}, u32[]{:S(2)}) copy-start(bf16[1,192,4096]{2,1,0:T(8,128)(2,1)} %get-tuple-element.28) | copy-start | bytes 4718596
  170.0 2.0 %copy-start = (bf16[1,192,4096]{2,1,0:T(8,128)(2,1)S(1)}, bf16[1,192,4096]{2,1,0:T(8,128)(2,1)}, u32[]{:S(2)}) copy-start(bf16[1,192,4096]{2,1,0:T(8,128)(2,1)} %get-tuple-element.29) | copy-start | bytes 4718596

commit v2 on v1

--- a/solution.py
+++ b/solution.py
@@ -31,9 +31,9 @@
 
 
 def kernel(
-    nz, tok, og, pp, wg, wu, wd,
-    tg_out, ext_out, gg_out, gu_out, gd_out,
-    pb, pm, pgm, ptm, ty, zs, xg, ww, acc, gp, up, hd, gpt, upt, hdt,
+    nz, tok, og, idt, gpr, wg, wu, wd,
+    tg_out, gate_out, gg_out, gu_out, gd_out,
+    pp, pb, pm, pgm, ptm, ty, zs, xg, ww, acc, gp, up, hd, gpt, upt, hdt,
     ps, pk, pr, hl, hr, fl, fr, rs, rz, ts, tr, go,
     pse, pke, pre, hle, hre, fle, fre, rse, rze, tse, tre,
     s_p, s_y, s_z, s_xl, s_xr, s_fl, s_fr, s_c, s_w,
@@ -79,11 +79,46 @@
     peers = [at_y(v) for v in y_peers] + [at_z(v) for v in z_peers] + [right, left, partner]
     for dev in peers:
         pl.semaphore_signal(barrier, inc=1, device_id=dev, device_id_type=MESH)
+
+    experts = nz * NY
+    few = nz * CAP
+    per_device = EXPERTS // experts
+
+    def iota(shape, dim):
+        return lax.broadcasted_iota(jnp.int32, shape, dim)
+
+    def ones(mask):
+        return jnp.where(mask, 1.0, 0.0)
+
+    cells = (toks, block_tokens)
+    place = ones(iota(cells, 1) == iota(cells, 0) + y * toks).astype(BF16)
+    ids = mm((idt[...].astype(F32) + 1.0).astype(BF16), place)
+    gates = mm(gpr[...], place)
+    wanted = (iota((experts, block_tokens), 0) * per_device + 1).astype(F32)
+    active = jnp.zeros((experts, block_tokens), F32)
+    weight = jnp.zeros((experts, block_tokens), F32)
+    for k in range(idt.shape[0]):
+        hit = ids[k : k + 1, :] == wanted
+        active = active + ones(hit)
+        weight = weight + jnp.where(hit, gates[k : k + 1, :], 0.0)
+    square = (block_tokens, block_tokens)
+    earlier = ones(iota(square, 0) < iota(square, 1)).astype(BF16)
+    rank = mm(active.astype(BF16), earlier)
+    ordinal = (active * (rank + 1.0)).astype(BF16)
+    weight = weight.astype(BF16)
+    number = (iota((few, block_tokens), 0) % CAP + 1).astype(F32)
+    target = iota((few, experts), 0) // CAP * NY
+    for v in range(NY):
+        select = ones(iota((few, experts), 1) == target + v).astype(BF16)
+        held = mm(select, ordinal) == number
+        pp[v, 0] = ones(held).astype(BF16)
+        pp[v, 1] = jnp.where(held, mm(select, weight), 0.0).astype(BF16)
+
     pl.semaphore_wait(barrier, len(peers))
-
+    table = rows_of(y, few)
     for v in y_peers:
-        send(pp.at[v], pb.at[y], t_p, s_p, at_y(v))
-    local(pp.at[y], pb.at[y], s_p)
+        send(pp.at[v], pb.at[:, table], t_p, s_p, at_y(v))
+    local(pp.at[y], pb.at[:, table], s_p)
 
     @pl.loop(0, chunks)
     def _(c):
@@ -100,14 +135,15 @@
         for i, src in enumerate((wg, wu, wd)):
             local(src.at[:, cols], ww.at[c, i], s_w)
 
+    acc[...] = jnp.zeros_like(acc)
     take(pb, s_p)
-    total = pb[0].astype(F32)
-    for v in range(1, NY):
-        total = total + pb[v].astype(F32)
-    pm[...] = total[0].astype(BF16)
-    pgm[...] = total[1].astype(BF16)
-    ptm[...] = total[0].T.astype(BF16)
-    acc[...] = jnp.zeros_like(acc)
+    slot = iota((block, block), 0)
+    source = slot // CAP % NY * few + slot // unit * CAP + slot % CAP
+    spread = ones(iota((block, block), 1) == source).astype(BF16)
+    chosen = mm(spread, pb[0])
+    pm[...] = chosen.astype(BF16)
+    pgm[...] = mm(spread, pb[1]).astype(BF16)
+    ptm[...] = chosen.T.astype(BF16)
 
     mine_rows = rows_of(core * NX + x, block)
     left_rows = rows_of(core * NX + xl, block)
@@ -168,11 +204,11 @@
             acc[1, rows] += mm_t(xs, ww[c, 1])
             acc[2, rows] += mm_t(xg[c, 1, rows], ww[c, 2])
 
-    stages = (stage_z, stage_x, stage_x2, stage_x3, stage_f)
-
-    @pl.loop(0, chunks + len(stages) - 1)
+    stages = ((0, stage_z), (2, stage_x), (5, stage_f), (3, stage_x2), (4, stage_x3))
+
+    @pl.loop(0, chunks + len(stages))
     def _(t):
-        for lag, stage in enumerate(stages):
+        for lag, stage in stages:
             c = t - lag
 
             @pl.when(jnp.logical_and(c >= 0, c < chunks))
@@ -269,7 +305,12 @@
         if refs is main:
             tg_out[:, rows_of(c, width)] = out.astype(BF16)
         else:
-            ext_out[...] = out
+            gate_terms = out.T
+            expert = iota((LANES, toks), 0) * per_device
+            for k in range(idt.shape[0]):
+                hit = idt[k : k + 1, :] == expert
+                term = jnp.sum(jnp.where(hit, gate_terms, 0.0), axis=0, keepdims=True)
+                gate_out[k : k + 1, :] = term / gpr[k : k + 1, :].astype(F32)
 
     def transposes():
         for src, dst in ((gp, gpt), (up, upt), (hd, hdt)):
@@ -292,10 +333,6 @@
 
     @pl.loop(0, chunks + len(returns))
     def _(t):
-        @pl.when(t < chunks)
-        def _():
-            stage_pair(t)
-
         for lag, stage in enumerate(returns):
             @pl.when(t == lag)
             def _(stage=stage):
@@ -307,15 +344,19 @@
             def _(stage=stage, c=c):
                 stage(main, c)
 
-        @pl.when(t == 0)
+        @pl.when(t < chunks)
+        def _():
+            stage_pair(t)
+
+        @pl.when(t == 2)
         def _():
             transposes()
 
-        @pl.when(t < chunks)
+        @pl.when(jnp.logical_and(t >= 3, t < chunks + 3))
         def _():
-            weight_grads(t)
-
-    take(pb.at[pl.ds(1, NY - 1)], t_p)
+            weight_grads(t - 3)
+
+    take(pb.at[:, pl.ds(0, (NY - 1) * few)], t_p)
 
     def drain(refs, c):
         b = pick(refs, c)
@@ -338,7 +379,7 @@
             pltpu.make_async_copy(go.at[c, i], dst.at[0, :, cols], u_o.at[c, i]).wait()
 
 
-def run(tokens, out_grad, pp, w_gate, w_up, w_down, nz):
+def run(tokens, out_grad, ids, gates, w_gate, w_up, w_down, nz):
     toks, depth = tokens.shape
     units = w_gate.shape[0]
     chunks = CHUNKS
@@ -367,7 +408,8 @@
         ]
 
     scratch = [
-        v((NY, 2, block, NY * toks), BF16),
+        v((NY, 2, nz * CAP, NY * toks), BF16),
+        v((2, block, NY * toks), BF16),
         v((block, NY * toks), BF16),
         v((block, NY * toks), BF16),
         v((NY * toks, block), BF16),
@@ -400,50 +442,55 @@
         body,
         out_shape=(
             jax.ShapeDtypeStruct((toks, depth), BF16),
-            jax.ShapeDtypeStruct((toks, LANES), F32),
+            jax.ShapeDtypeStruct(gates.shape, F32),
             grads, grads, grads,
         ),
-        in_specs=[any_spec] * 6,
+        in_specs=[any_spec] * 2 + [vmem_spec] * 2 + [any_spec] * 3,
         out_specs=(vmem_spec, vmem_spec, any_spec, any_spec, any_spec),
         scratch_shapes=scratch,
         compiler_params=pltpu.CompilerParams(
             collective_id=0, has_side_effects=True, vmem_limit_bytes=67043328
         ),
-    )(tokens, out_grad, pp, w_gate, w_up, w_down)
+    )(tokens, out_grad, ids, gates, w_gate, w_up, w_down)
+
+
+def place_kernel(*refs):
+    n = (len(refs) - 2) // 3
+    srcs, dsts, bufs = refs[:n], refs[n : 2 * n], refs[2 * n : 3 * n]
+    came, left = refs[3 * n :]
+    for i in range(n):
+        pltpu.make_async_copy(srcs[i], bufs[i], came.at[i]).start()
+    for i in range(n):
+        pltpu.make_async_copy(srcs[i], bufs[i], came.at[i]).wait()
+        pltpu.make_async_copy(bufs[i], dsts[i], left.at[i]).start()
+    for i in range(n):
+        pltpu.make_async_copy(bufs[i], dsts[i], left.at[i]).wait()
+
+
+def place(*arrays):
+    any_spec = pl.BlockSpec(memory_space=pl.ANY)
+    return pl.pallas_call(
+        place_kernel,
+        out_shape=tuple(jax.ShapeDtypeStruct(a.shape, a.dtype) for a in arrays),
+        in_specs=[any_spec] * len(arrays),
+        out_specs=[any_spec] * len(arrays),
+        scratch_shapes=[
+            *[pltpu.VMEM(a.shape, a.dtype) for a in arrays],
+            pltpu.SemaphoreType.DMA((len(arrays),)),
+            pltpu.SemaphoreType.DMA((len(arrays),)),
+        ],
+    )(*arrays)
 
 
 def body(tokens, out_grad, gate_probs, route_ids, w_gate, w_up, w_down):
-    n_targets = lax.axis_size("expert")
-    nz = n_targets // NY
-    toks = tokens.shape[0]
-    per_device = EXPERTS // n_targets
-    y = lax.rem(lax.axis_index("expert"), NY)
-    gates = gate_probs.astype(F32)
-    named = route_ids[:, :, None] == per_device * jnp.arange(n_targets, dtype=jnp.int32)
-    active = jnp.any(named, axis=1).astype(F32)
-    weight = jnp.sum(jnp.where(named, gates[:, :, None], 0.0), axis=1)
-    order = jnp.arange(toks)
-    before = (order[:, None] > order[None, :]).astype(F32)
-    rank = jnp.dot(before, active, preferred_element_type=F32)
-    placed = jnp.logical_and(
-        active.T[:, None, :] > 0.0,
-        rank.T[:, None, :] == jnp.arange(CAP, dtype=F32)[None, :, None],
+    nz = lax.axis_size("expert") // NY
+    token_grad, gate_grad, grad_gate, grad_up, grad_down = run(
+        tokens, out_grad, route_ids.T, gate_probs.T, w_gate[0], w_up[0], w_down[0], nz
     )
-    one = placed.astype(F32)
-    scaled = jnp.where(placed, weight.T[:, None, :], 0.0)
-    both = jnp.stack([one, scaled]).reshape(2, nz, NY, CAP, toks)
-    mine = (jnp.arange(NY) == y).astype(F32)
-    spread = (
-        both.transpose(2, 0, 1, 3, 4)[:, :, :, None, :, None, :]
-        * mine[None, None, None, :, None, None, None]
-        * mine[None, None, None, None, None, :, None]
+    token_grad, grad_gate, grad_up, grad_down = place(
+        token_grad, grad_gate, grad_up, grad_down
     )
-    pp = spread.reshape(NY, 2, nz * NY * CAP, NY * toks).astype(BF16)
-    token_grad, ext, grad_gate, grad_up, grad_down = run(
-        tokens, out_grad, pp, w_gate[0], w_up[0], w_down[0], nz
-    )
-    values = jnp.sum(jnp.where(named, ext[:, None, :n_targets], 0.0), axis=2)
-    return token_grad, values / gates, grad_gate, grad_up, grad_down
+    return token_grad, gate_grad.T, grad_gate, grad_up, grad_down
 
 
 def solution(mesh):

time: 174 us -> 164 us (0.943)
  local copies, waits for them, and re-layouts: 11.7 us -> 0.6 us
  Pallas kernels: 158 us -> 161 us
  other arithmetic: 2.94 us -> 0 us
    unnamed x17 -> x3, local copies, waits for them, and re-layouts: 9.82 us -> 0.6 us
    pallas_call x0 -> x1, Pallas kernels: none -> 3.92 us  [place(): pl.pallas_call(place_kernel, out_shape=tuple((jax.ShapeDtypeStruct(a.shap...]
where the time goes in v2:
time: 164 us; the launch traced here: 163 us
  Pallas kernels  161 us (98%)
    pallas_call x1, Pallas kernels, run(): pl.pallas_call(body, out_shape=(jax.ShapeDtypeStruct((toks, depth), BF16)...  158 us
    pallas_call x1, Pallas kernels, place(): pl.pallas_call(place_kernel, out_shape=tuple((jax.ShapeDtypeStruct(a.shap...  3.92 us

profile of v2, /device:TPU:16, one launch (start us, length us, event | category | flops | bytes accessed | tf_op | source)
XLA Modules:
  0.0 162.7 jit_solution(1428236217221047511)
XLA Ops:
  0.6 157.6 %shard_map.110 = (bf16[32,4096]{1,0:T(8,128)(2,1)}, f32[8,32]{1,0:T(8,128)}, bf16[1,192,4096]{2,1,0:T(8,128)(2,1)}, bf16[1,192,4096]{2,1,0:T(8,128)(2,1)}, bf16[1,192,4096]{2,1,0:T(8,128)(2,1)}) custom-call(bf16[32,4096]{1,0:T(8,128)(2,1)} %refs_0_.1, bf16[32,4096]{1,0:T(8,128)(2,1)} %refs_1_.1, s32[8,32]{1,0:T(8,128)} %bitcast.10, bf16[8,32]{1,0:T(8,128)(2,1)} %bitcast.11, ...), custom_call_target="tpu_custom_call" | custom-call | tf_op jit(solution)/shard_map/pallas_call | solution.py:441
  158.2 0.0 copy-start
  158.2 3.9 %shard_map.111 = (bf16[32,4096]{1,0:T(8,128)(2,1)}, bf16[1,192,4096]{2,1,0:T(8,128)(2,1)}, bf16[1,192,4096]{2,1,0:T(8,128)(2,1)}, bf16[1,192,4096]{2,1,0:T(8,128)(2,1)}) custom-call(bf16[32,4096]{1,0:T(8,128)(2,1)} %get-tuple-element.14.refs_0_, bf16[1,192,4096]{2,1,0:T(8,128)(2,1)} %get-tuple-element.15.refs_1_, ...), custom_call_target="tpu_custom_call" | custom-call | tf_op jit(solution)/shard_map/pallas_call | solution.py:472
  162.1 0.0 copy-done
  162.2 0.6 copy.13
Async XLA Ops:
  158.2 3.9 %copy-start = (f32[8,32]{1,0:T(8,128)S(1)}, f32[8,32]{1,0:T(8,128)}, u32[]{:S(2)}) copy-start(f32[8,32]{1,0:T(8,128)} %get-tuple-element.19) | copy-start | bytes 3076

commit v3 on v2

--- a/solution.py
+++ b/solution.py
@@ -10,7 +10,8 @@
 NX = 4
 NC = 2
 NY = 4
-CHUNKS = 8
+CHUNKS = 16
+PIECES = 6
 LANES = 128
 MESH = pl.DeviceIdType.MESH
 LAST = (((1,), (1,)), ((), ()))
@@ -34,12 +35,12 @@
     nz, tok, og, idt, gpr, wg, wu, wd,
     tg_out, gate_out, gg_out, gu_out, gd_out,
     pp, pb, pm, pgm, ptm, ty, zs, xg, ww, acc, gp, up, hd, gpt, upt, hdt,
-    ps, pk, pr, hl, hr, fl, fr, rs, rz, ts, tr, go,
+    ps, pk, pr, hl, hr, fl, fr, rs, rz, ts, tr, go, tg,
     pse, pke, pre, hle, hre, fle, fre, rse, rze, tse, tre,
     s_p, s_y, s_z, s_xl, s_xr, s_fl, s_fr, s_c, s_w,
     t_p, t_y, t_z, t_x,
     r_c, r_hl, r_hr, r_fl, r_fr, r_z, r_y,
-    u_c, u_h, u_f, u_z, u_y, u_o,
+    u_c, u_h, u_f, u_z, u_y, u_o, u_t,
 ):
     chunks, _, block_tokens, width = ty.shape
     toks = block_tokens // NY
@@ -204,9 +205,9 @@
             acc[1, rows] += mm_t(xs, ww[c, 1])
             acc[2, rows] += mm_t(xg[c, 1, rows], ww[c, 2])
 
-    stages = ((0, stage_z), (2, stage_x), (5, stage_f), (3, stage_x2), (4, stage_x3))
-
-    @pl.loop(0, chunks + len(stages))
+    stages = ((0, stage_z), (3, stage_x), (9, stage_f), (5, stage_x2), (7, stage_x3))
+
+    @pl.loop(0, chunks + 9)
     def _(t):
         for lag, stage in stages:
             c = t - lag
@@ -232,7 +233,6 @@
     @pl.loop(0, NX)
     def _(b):
         pse[rows_of(b, block)] = activate(rows_of(other * NX + b, block))
-        pke[rows_of(b, block)] = activate(rows_of(core * NX + b, block))
 
     main = (ps, pk, pr, hl, hr, fl, fr, rs, rz, ts, tr)
     extra = (pse, pke, pre, hle, hre, fle, fre, rse, rze, tse, tre)
@@ -244,10 +244,12 @@
         b = pick(refs, c)
         send(b[0], b[2], u_c.at[c], r_c.at[c], partner)
 
-    def stage_pair(c):
+    def pair_send(c):
         rows = rows_of(other, column)
         ps[c] = (mm(gp[rows], ww[c, 0]) + mm(up[rows], ww[c, 1])).astype(BF16)
         to_partner(main, c)
+
+    def pair_keep(c):
         rows = rows_of(core, column)
         pk[c] = (mm(gp[rows], ww[c, 0]) + mm(up[rows], ww[c, 1])).astype(BF16)
 
@@ -303,7 +305,8 @@
         for v in range(1, NY):
             out = out + summed[pl.ds(v * toks, toks)].astype(F32)
         if refs is main:
-            tg_out[:, rows_of(c, width)] = out.astype(BF16)
+            tg[c] = out.astype(BF16)
+            local(tg.at[c], tg_out.at[:, rows_of(c, width)], u_t.at[c])
         else:
             gate_terms = out.T
             expert = iota((LANES, toks), 0) * per_device
@@ -328,35 +331,20 @@
         for i, dst in enumerate((gg_out, gu_out, gd_out)):
             local(go.at[c, i], dst.at[0, :, cols], u_o.at[c, i])
 
+    pair_send(0)
     to_partner(extra, chunks)
-    returns = (stage_r1, stage_r2, stage_r3, stage_r4, stage_r5)
-
-    @pl.loop(0, chunks + len(returns))
-    def _(t):
-        for lag, stage in enumerate(returns):
-            @pl.when(t == lag)
-            def _(stage=stage):
-                stage(extra, chunks)
-
-            c = t - lag - 1
-
-            @pl.when(jnp.logical_and(c >= 0, c < chunks))
-            def _(stage=stage, c=c):
-                stage(main, c)
-
-        @pl.when(t < chunks)
-        def _():
-            stage_pair(t)
-
-        @pl.when(t == 2)
-        def _():
-            transposes()
-
-        @pl.when(jnp.logical_and(t >= 3, t < chunks + 3))
-        def _():
-            weight_grads(t - 3)
-
-    take(pb.at[:, pl.ds(0, (NY - 1) * few)], t_p)
+
+    @pl.loop(0, NX)
+    def _(b):
+        pke[rows_of(b, block)] = activate(rows_of(core * NX + b, block))
+
+    returns = ((3, stage_r1), (6, stage_r2), (9, stage_r3), (12, stage_r4), (15, stage_r5))
+    turn = 9
+
+    def grads_out(c):
+        cols = rows_of(c, width)
+        for i, dst in enumerate((gg_out, gu_out, gd_out)):
+            pltpu.make_async_copy(go.at[c, i], dst.at[0, :, cols], u_o.at[c, i]).wait()
 
     def drain(refs, c):
         b = pick(refs, c)
@@ -366,17 +354,64 @@
         take(b[8].at[pl.ds(0, block - unit)], u_z.at[c])
         take(b[10].at[pl.ds(0, block_tokens - toks)], u_y.at[c])
 
+    @pl.loop(0, chunks + returns[-1][0])
+    def _(t):
+        for lag, stage in returns:
+            @pl.when(t == lag - 1)
+            def _(stage=stage):
+                stage(extra, chunks)
+
+            c = t - lag
+
+            @pl.when(jnp.logical_and(c >= 0, c < chunks))
+            def _(stage=stage, c=c):
+                stage(main, c)
+
+        @pl.when(t < chunks)
+        def _():
+            pair_keep(t)
+
+        @pl.when(t < chunks - 1)
+        def _():
+            pair_send(t + 1)
+
+        @pl.when(t == turn)
+        def _():
+            transposes()
+
+        @pl.when(jnp.logical_and(t > turn, t <= chunks // 2 + turn))
+        def _():
+            weight_grads(2 * (t - turn) - 2)
+            weight_grads(2 * (t - turn) - 1)
+
+        @pl.when(jnp.logical_and(t > turn + 2, t <= chunks // 2 + turn + 2))
+        def _():
+            grads_out(2 * (t - turn - 2) - 2)
+            grads_out(2 * (t - turn - 2) - 1)
+
+        @pl.when(t < chunks)
+        def _():
+            take(ty.at[t, :, pl.ds(0, block_tokens - toks)], t_y.at[t])
+            take(zs.at[t, :, pl.ds(0, block - unit)], t_z.at[t])
+            take(xg.at[t, :, pl.ds(0, 7 * block)], t_x.at[t])
+
+        done = t - returns[-1][0] - 1
+
+        @pl.when(done >= 0)
+        def _():
+            drain(main, done)
+            pltpu.make_async_copy(
+                tg.at[done], tg_out.at[:, rows_of(done, width)], u_t.at[done]
+            ).wait()
+
+    take(pb.at[:, pl.ds(0, (NY - 1) * few)], t_p)
+
     drain(extra, chunks)
 
-    @pl.loop(0, chunks)
+    @pl.loop(chunks - 1, chunks)
     def _(c):
-        take(ty.at[c, :, pl.ds(0, block_tokens - toks)], t_y.at[c])
-        take(zs.at[c, :, pl.ds(0, block - unit)], t_z.at[c])
-        take(xg.at[c, :, pl.ds(0, 7 * block)], t_x.at[c])
         drain(main, c)
-        cols = rows_of(c, width)
-        for i, dst in enumerate((gg_out, gu_out, gd_out)):
-            pltpu.make_async_copy(go.at[c, i], dst.at[0, :, cols], u_o.at[c, i]).wait()
+        pltpu.make_async_copy(tg.at[c], tg_out.at[:, rows_of(c, width)], u_t.at[c]).wait()
 
 
 def run(tokens, out_grad, ids, gates, w_gate, w_up, w_down, nz):
@@ -426,12 +461,14 @@
         v((units, total), BF16),
         *back((chunks,), width),
         v((chunks, 3, units, width), BF16),
+        v((chunks, toks, width), BF16),
         *back((), LANES),
         dma(()), *[dma((chunks,)) for _ in range(7)], dma(()),
         dma(()), *[dma((chunks,)) for _ in range(3)],
         *[dma((chunks + 1,)) for _ in range(7)],
         *[dma((chunks + 1,)) for _ in range(5)],
         dma((chunks, 3)),
+        dma((chunks,)),
     ]
     grads = jax.ShapeDtypeStruct((1, units, depth), BF16)
 
@@ -446,7 +483,7 @@
             grads, grads, grads,
         ),
         in_specs=[any_spec] * 2 + [vmem_spec] * 2 + [any_spec] * 3,
-        out_specs=(vmem_spec, vmem_spec, any_spec, any_spec, any_spec),
+        out_specs=(any_spec, vmem_spec, any_spec, any_spec, any_spec),
         scratch_shapes=scratch,
         compiler_params=pltpu.CompilerParams(
             collective_id=0, has_side_effects=True, vmem_limit_bytes=67043328
@@ -458,13 +495,20 @@
     n = (len(refs) - 2) // 3
     srcs, dsts, bufs = refs[:n], refs[n : 2 * n], refs[2 * n : 3 * n]
     came, left = refs[3 * n :]
+    jobs = []
     for i in range(n):
-        pltpu.make_async_copy(srcs[i], bufs[i], came.at[i]).start()
-    for i in range(n):
-        pltpu.make_async_copy(srcs[i], bufs[i], came.at[i]).wait()
-        pltpu.make_async_copy(bufs[i], dsts[i], left.at[i]).start()
-    for i in range(n):
-        pltpu.make_async_copy(bufs[i], dsts[i], left.at[i]).wait()
+        rows = srcs[i].shape[-2]
+        step = max(32, rows // PIECES)
+        for low in range(0, rows, step):
+            piece = (slice(None),) * (len(srcs[i].shape) - 2) + (pl.ds(low, step),)
+            jobs.append((srcs[i].at[piece], bufs[i].at[piece], dsts[i].at[piece]))
+    for k, (src, buf, _) in enumerate(jobs):
+        pltpu.make_async_copy(src, buf, came.at[k]).start()
+    for k, (src, buf, dst) in enumerate(jobs):
+        pltpu.make_async_copy(src, buf, came.at[k]).wait()
+        pltpu.make_async_copy(buf, dst, left.at[k]).start()
+    for k, (_, buf, dst) in enumerate(jobs):
+        pltpu.make_async_copy(buf, dst, left.at[k]).wait()
 
 
 def place(*arrays):
@@ -476,8 +520,8 @@
         out_specs=[any_spec] * len(arrays),
         scratch_shapes=[
             *[pltpu.VMEM(a.shape, a.dtype) for a in arrays],
-            pltpu.SemaphoreType.DMA((len(arrays),)),
-            pltpu.SemaphoreType.DMA((len(arrays),)),
+            pltpu.SemaphoreType.DMA((len(arrays) * PIECES,)),
+            pltpu.SemaphoreType.DMA((len(arrays) * PIECES,)),
         ],
     )(*arrays)
 

time: 164 us -> 154 us (0.939)
  Pallas kernels: 161 us -> 153 us
    pallas_call x1, Pallas kernels: 158 us -> 148 us  [run(): pl.pallas_call(body, out_shape=(jax.ShapeDtypeStruct((toks, depth), BF16)...]
where the time goes in v3:
time: 154 us
  Pallas kernels  153 us (99%)
    pallas_call x1, Pallas kernels, run(): pl.pallas_call(body, out_shape=(jax.ShapeDtypeStruct((toks, depth), BF16)...  148 us
    pallas_call x1, Pallas kernels, place(): pl.pallas_call(place_kernel, out_shape=tuple((jax.ShapeDtypeStruct(a.shap...  4.8 us

profile of v3, /device:TPU:16, one launch (start us, length us, event | category | flops | bytes accessed | tf_op | source)
XLA Modules:
  0.0 154.1 jit_solution(15927724274731094338)
XLA Ops:
  0.6 148.0 %shard_map.110 = (bf16[32,4096]{1,0:T(8,128)(2,1)}, f32[8,32]{1,0:T(8,128)}, bf16[1,192,4096]{2,1,0:T(8,128)(2,1)}, bf16[1,192,4096]{2,1,0:T(8,128)(2,1)}, bf16[1,192,4096]{2,1,0:T(8,128)(2,1)}) custom-call(bf16[32,4096]{1,0:T(8,128)(2,1)} %refs_0_.1, bf16[32,4096]{1,0:T(8,128)(2,1)} %refs_1_.1, s32[8,32]{1,0:T(8,128)} %bitcast.10, bf16[8,32]{1,0:T(8,128)(2,1)} %bitcast.11, ...), custom_call_target="tpu_custom_call" | custom-call | tf_op jit(solution)/shard_map/pallas_call | solution.py:478
  148.6 0.0 copy-start
  148.7 4.8 %shard_map.111 = (bf16[32,4096]{1,0:T(8,128)(2,1)}, bf16[1,192,4096]{2,1,0:T(8,128)(2,1)}, bf16[1,192,4096]{2,1,0:T(8,128)(2,1)}, bf16[1,192,4096]{2,1,0:T(8,128)(2,1)}) custom-call(bf16[32,4096]{1,0:T(8,128)(2,1)} %get-tuple-element.14.refs_0_, bf16[1,192,4096]{2,1,0:T(8,128)(2,1)} %get-tuple-element.15.refs_1_, ...), custom_call_target="tpu_custom_call" | custom-call | tf_op jit(solution)/shard_map/pallas_call | solution.py:516
  153.5 0.0 copy-done
  153.5 0.6 copy.13
Async XLA Ops:
  148.6 4.8 %copy-start = (f32[8,32]{1,0:T(8,128)S(1)}, f32[8,32]{1,0:T(8,128)}, u32[]{:S(2)}) copy-start(f32[8,32]{1,0:T(8,128)} %get-tuple-element.19) | copy-start | bytes 3076

commit v4 on v3

--- a/solution.py
+++ b/solution.py
@@ -11,7 +11,7 @@
 NC = 2
 NY = 4
 CHUNKS = 16
-PIECES = 6
+PIECES = 1
 LANES = 128
 MESH = pl.DeviceIdType.MESH
 LAST = (((1,), (1,)), ((), ()))

time: 154 us -> 153 us (level)
  no operation moved by 1% of the time
where the time goes in v4:
time: 153 us
  Pallas kernels  152 us (99%)
    pallas_call x1, Pallas kernels, run(): pl.pallas_call(body, out_shape=(jax.ShapeDtypeStruct((toks, depth), BF16)...  148 us
    pallas_call x1, Pallas kernels, place(): pl.pallas_call(place_kernel, out_shape=tuple((jax.ShapeDtypeStruct(a.shap...  3.92 us

profile of v4, /device:TPU:16, one launch (start us, length us, event | category | flops | bytes accessed | tf_op | source)
XLA Modules:
  0.0 153.2 jit_solution(15741959959396465768)
XLA Ops:
  0.6 148.0 %shard_map.110 = (bf16[32,4096]{1,0:T(8,128)(2,1)}, f32[8,32]{1,0:T(8,128)}, bf16[1,192,4096]{2,1,0:T(8,128)(2,1)}, bf16[1,192,4096]{2,1,0:T(8,128)(2,1)}, bf16[1,192,4096]{2,1,0:T(8,128)(2,1)}) custom-call(bf16[32,4096]{1,0:T(8,128)(2,1)} %refs_0_.1, bf16[32,4096]{1,0:T(8,128)(2,1)} %refs_1_.1, s32[8,32]{1,0:T(8,128)} %bitcast.10, bf16[8,32]{1,0:T(8,128)(2,1)} %bitcast.11, ...), custom_call_target="tpu_custom_call" | custom-call | tf_op jit(solution)/shard_map/pallas_call | solution.py:478
  148.6 0.0 copy-start
  148.7 3.9 %shard_map.111 = (bf16[32,4096]{1,0:T(8,128)(2,1)}, bf16[1,192,4096]{2,1,0:T(8,128)(2,1)}, bf16[1,192,4096]{2,1,0:T(8,128)(2,1)}, bf16[1,192,4096]{2,1,0:T(8,128)(2,1)}) custom-call(bf16[32,4096]{1,0:T(8,128)(2,1)} %get-tuple-element.14.refs_0_, bf16[1,192,4096]{2,1,0:T(8,128)(2,1)} %get-tuple-element.15.refs_1_, ...), custom_call_target="tpu_custom_call" | custom-call | tf_op jit(solution)/shard_map/pallas_call | solution.py:516
  152.6 0.0 copy-done
  152.6 0.6 copy.13
Async XLA Ops:
  148.6 3.9 %copy-start = (f32[8,32]{1,0:T(8,128)S(1)}, f32[8,32]{1,0:T(8,128)}, u32[]{:S(2)}) copy-start(f32[8,32]{1,0:T(8,128)} %get-tuple-element.19) | copy-start | bytes 3076
